TPU v7x, 256 devices: a whole 4x4x8 slice. The times are simulated.
256 devices in a mesh: group: 8 (over x, core), member: 32 (over y, z).
Axes of the slice: x: 4, y: 4, z: 8, core: 2. Of those that a mesh axis runs over, the one named last changes fastest.
Arguments:
- q_rows: bfloat16 [65536, 8192], P(('group', 'member')), may hold values from -36 to 36
- own_kv: bfloat16 [65536, 1024], P(('group', 'member')), may hold values from -6 to 6
- cache: bfloat16 [1024, 64, 1024], P(('group', 'member')), may hold values from -6 to 6
- recomp_hidden: bfloat16 [512, 8, 16, 4096], P(('group', 'member')), may hold values from -6 to 6
- w_kv: bfloat16 [4096, 1024], P('member', 'group'), may hold values from -0.09375 to 0.09375
- retrieval: int32 [512, 8], P(('group', 'member')), may hold values from 0 to 127, as said below
- positions: int32 [512, 8, 16], P(('group', 'member')), may hold values from 0 to 63, as said below
Outputs:
- attn_out: bfloat16 [65536, 8192], P(('group', 'member'))
Inputs may be any that keep to these rules, and one draw needn't show every extreme that they name: `retrieval`: the 8 passages of one query are different. Passage i of a group's corpus is held by the device of member index i // 4 in that group. The queries of one device name at most 1 passages held by any one device, and this bound is reached. The 16 positions of one retrieved passage are different.
All inputs are finite; a program needn't handle non-finite values.
Results may differ from a plain program's by a relative error of at most 0.0054.
Values may be sent and summed in bfloat16 or wider, within the bound.
A program may use at most 128 MiB of HBM per device.

v0:
```python
import jax
import jax.numpy as jnp
from jax import lax
from jax.sharding import PartitionSpec as P

D = 4096
HQ = 64
KVH = 4
HD = 128
TOPP = 8
QLEN = 128
PLEN = 64
RECOMP = 16
EPSILON = 1e-06


def local(q_rows, own_kv, cache, recomp_hidden, w_kv, retrieval, positions):
    query_count = retrieval.shape[0]
    requests = query_count * TOPP
    kv_width = 2 * KVH * HD
    grouped = HQ // KVH
    span_keys = TOPP * PLEN + QLEN
    scale = 1.0 / HD**0.5
    row_count = requests * RECOMP
    hidden = recomp_hidden.reshape(row_count, D).astype(jnp.float32)
    normed = (
        hidden * lax.rsqrt(jnp.mean(hidden * hidden, axis=1, keepdims=True) + EPSILON)
    ).astype(jnp.bfloat16)
    head_columns = lax.all_gather(w_kv, "group", axis=1, tiled=True)
    projected = jnp.dot(
        normed,
        lax.all_gather(head_columns, "member", axis=0, tiled=True),
        preferred_element_type=jnp.float32,
    )
    recomputed = projected.astype(jnp.bfloat16).reshape(requests, RECOMP, kv_width)
    wanted = retrieval.reshape(requests)
    pass_local = cache.shape[0]
    holders_count = lax.axis_size("member")
    my_index = lax.axis_index("member")
    capacity = -(-requests // holders_count)
    request_table = lax.all_gather(wanted.reshape(1, requests), "member", axis=0, tiled=True)
    mine_mask = request_table // pass_local == my_index
    earlier_mask = (jnp.arange(requests)[:, None] < jnp.arange(requests)[None, :]).astype(jnp.int32)
    slot_rank = jnp.dot(mine_mask.astype(jnp.int32), earlier_mask)
    slot_table = mine_mask[:, None, :] & (
        slot_rank[:, None, :] == jnp.arange(capacity)[None, :, None]
    )
    local_index = jnp.sum(
        jnp.where(slot_table, (request_table % pass_local)[:, None, :], 0), axis=2
    )
    slot_filled = jnp.any(slot_table, axis=2)
    outgoing = jnp.where(
        slot_filled[:, :, None, None], cache[local_index], jnp.zeros((), cache.dtype)
    )
    arrived = lax.all_to_all(outgoing, "member", split_axis=0, concat_axis=0, tiled=True)
    holder_of = wanted // pass_local
    same_holder = holder_of[:, None] == holder_of[None, :]
    before_me = jnp.arange(requests)[None, :] < jnp.arange(requests)[:, None]
    copy_rank = jnp.sum((same_holder & before_me).astype(jnp.int32), axis=1)
    blocks = arrived.reshape(holders_count * capacity, PLEN, kv_width)[
        holder_of * capacity + copy_rank
    ]
    spots = positions.reshape(requests, RECOMP)
    onehot = spots[:, :, None] == jnp.arange(PLEN)[None, None, :]
    covered = jnp.any(onehot, axis=1)
    placed = jnp.einsum(
        "krp,kre->kpe", onehot.astype(jnp.bfloat16), recomputed, preferred_element_type=jnp.float32
    ).astype(jnp.bfloat16)
    context = jnp.where(covered[:, :, None], placed, blocks).reshape(
        query_count, TOPP * PLEN, kv_width
    )
    context = jnp.concatenate([context, own_kv.reshape(query_count, QLEN, kv_width)], axis=1)
    keys = context[:, :, : KVH * HD].reshape(query_count, span_keys, KVH, HD)
    values = context[:, :, KVH * HD :].reshape(query_count, span_keys, KVH, HD)
    queries = q_rows.reshape(query_count, QLEN, KVH, grouped, HD)
    token_pos = jnp.arange(QLEN)[:, None]
    key_pos = jnp.arange(span_keys)[None, :]
    visible = (key_pos < TOPP * PLEN) | (key_pos - TOPP * PLEN <= token_pos)

    def attend(operands):
        query_block, key_block, value_block = operands
        scores = (
            jnp.einsum("tkgd,skd->kgts", query_block, key_block, preferred_element_type=jnp.float32)
            * scale
        )
        scores = jnp.where(visible, scores, -jnp.inf)
        peak = jnp.max(scores, axis=-1, keepdims=True)
        expd = jnp.exp(scores - peak)
        probs = (expd / jnp.sum(expd, axis=-1, keepdims=True)).astype(jnp.bfloat16)
        output = jnp.einsum(
            "kgts,skd->tkgd", probs, value_block, preferred_element_type=jnp.float32
        )
        return output.astype(jnp.bfloat16).reshape(QLEN, HQ * HD)

    results = lax.map(attend, (queries, keys, values))
    return results.reshape(query_count * QLEN, HQ * HD)


def solution(mesh):
    placed = (
        P(("group", "member"), None),
        P(("group", "member"), None),
        P(("group", "member"), None, None),
        P(("group", "member"), None, None, None),
        P("member", "group"),
        P(("group", "member"), None),
        P(("group", "member"), None, None),
    )
    return jax.shard_map(
        local, mesh=mesh, in_specs=placed, out_specs=P(("group", "member"), None), check_vma=False
    )
```

profile of v0, /device:TPU:32, one launch (start us, length us, event | category | flops | bytes accessed | tf_op | source)
XLA Modules:
  0.0 287.2 jit_solution(2852515802772880683)
XLA Ops:
  6.5 13.6 %all_gather.9 = bf16[128,1024]{1,0:T(8,128)(2,1)} all-gather(bf16[128,128]{1,0:T(8,128)(2,1)} %param.13), channel_id=1, replica_groups=mesh['group'=8,'member'=32] {'group'}, dimensions={1}, use_global_device_ids=true | all-gather | bytes 294912 | tf_op jit(solution)/shard_map/all_gather | solution.py:29
  21.0 40.2 %all-gather = s32[32,1,16]{2,1,0:T(1,128)S(1)} all-gather(s32[1,1,16]{2,1,0:T(1,128)S(1)} %reshape.252), channel_id=1, replica_groups=mesh['group'=8,'member'=32] {'member'}, dimensions={0}, use_global_device_ids=true | all-gather | bytes 2112 | tf_op jit(solution)/shard_map/all_gather | solution.py:41
  61.5 2.8 gather_fusion
  64.4 4.5 %bitcast_select_fusion.4 = bf16[32,1,64,1024]{3,2,1,0:T(8,128)(2,1)} fusion(bf16[32,64,1024]{2,1,0:T(8,128)(2,1)} %gather_fusion, pred[32]{0:T(512)(128)(4,1)S(1)} %reduce_or.19), kind=kLoop, calls=%fused_computation.31 | loop fusion | flops 2097152 | bytes 8388640 | tf_op jit(solution)/shard_map/jit(_where)/select_n | solution.py:52
  68.9 8.1 %all-to-all-start = ((bf16[32,1,64,1024]{3,2,1,0:T(8,128)(2,1)}), bf16[32,1,64,1024]{3,2,1,0:T(8,128)(2,1)}, u32[]{:S(2)}, u32[]{:S(2)}) async-start(bf16[32,1,64,1024]{3,2,1,0:T(8,128)(2,1)} %bitcast_select_fusion.4), calls=%async_computation | async-start | bytes 8388608 | tf_op jit(solution)/shard_map/all_to_all | solution.py:55
  78.1 5.4 %copy.46 = bf16[32,8,64,128]{3,2,1,0:T(8,128)(2,1)} copy(bf16[32,8,64,128]{3,1,2,0:T(8,128)(2,1)} %bitcast.134) | data formatting | bytes 8388608
  83.8 1.9 fusion.30
  85.7 118.0 %all-to-all-done = bf16[32,1,64,1024]{3,2,1,0:T(8,128)(2,1)} async-done(((bf16[32,1,64,1024]{3,2,1,0:T(8,128)(2,1)}), bf16[32,1,64,1024]{3,2,1,0:T(8,128)(2,1)}, u32[]{:S(2)}, u32[]{:S(2)}) %all-to-all-start) | async-done | bytes 4194336 | tf_op jit(solution)/shard_map/all_to_all | solution.py:55
  203.7 2.9 gather_fusion.1
  206.6 6.3 %convolution_convert_fusion = bf16[256,1024]{1,0:T(8,128)(2,1)S(1)} fusion(bf16[256,4096]{1,0:T(8,128)(2,1)} %fusion.30, bf16[4096,1024]{1,0:T(8,128)(2,1)} %all-gather.3.cloned.1.call-done), kind=kOutput, calls=%fused_computation.40 | convolution fusion | flops 2147745792 | bytes 11010048 | tf_op jit(solution)/shard_map/dot_general | solution.py:30
  213.0 2.6 convert_select_fusion
  215.6 2.9 copy.34
  218.4 1.7 pad_maximum_fusion
  220.2 59.2 %while.11 = (s32[]{:T(128)}, bf16[2,128,8192]{2,1,0:T(8,128)(2,1)}, bf16[2,640,4,128]{1,3,2,0:T(8,128)(2,1)}, bf16[2,640,4,128]{1,3,2,0:T(8,128)(2,1)}, bf16[2,1...) while((s32[]{:T(128)}, bf16[2,128,8192]{2,1,0:T(8,128)(2,1)}, ...), condition=%wide.region_8.9_spmd.clone, body=%wide.region_5.8_spmd.clone.sunk | while | flops 2717024768 | bytes 60265176 | solution.py:95
  220.2 2.0 constant_dynamic-slice_fusion.2
  222.4 12.5 %fusion.73 = (f32[4,16,128]{2,1,0:T(8,128)S(1)}, f32[4,16,128,640]{2,3,1,0:T(8,128)}) fusion(pred[128,640]{0,1:T(8,128)(4,1)S(1)} %fusion.72, bf16[1,128,4,16,128]{4,3,2,1,0:T(8,128)(2,1)S(1)} %constant_dynamic-slice_fusion.2, bf16[2,640,4,128]{1,3,2,0:T(8,128)(2,1)} %get-tuple-element.170, s32[]{:T(128)} %get-tuple-element.159), kind=kOutput, calls=%fused_computation.92.clone.1 | convolution fusion | flops 1363149440 | bytes 23839232 | tf_op jit(solution)/shard_map/while/body/eval_jaxpr/sub | solution.py:88
  234.9 10.4 %fusion.74 = bf16[4,128,16,128]{3,1,2,0:T(8,128)(2,1)} fusion(f32[4,16,128,640]{2,3,1,0:T(8,128)} %get-tuple-element.149, f32[4,16,128]{2,1,0:T(8,128)S(1)} %get-tuple-element.150, bf16[2,640,4,128]{1,3,2,0:T(8,128)(2,1)} %get-tuple-element.169, s32[]{:T(128)} %get-tuple-element.159), kind=kOutput, calls=%fused_computation.14.clone.1 | convolution fusion | flops 1353711616 | bytes 23757312 | tf_op jit(solution)/shard_map/while/body/eval_jaxpr/kgts,skd->tkgd/dot_general | solution.py:90
  245.4 2.9 %copy.61 = bf16[1,128,8192]{2,1,0:T(8,128)(2,1)S(1)} copy(bf16[1,128,8192]{1,2,0:T(8,128)(2,1)} %bitcast.131) | data formatting | bytes 4194304 | tf_op jit(solution)/shard_map/while/body/jit(dynamic_update_index_in_dim)/dynamic_update_slice | solution.py:95
  248.3 1.5 constant_dynamic-update-slice_fusion.2
  249.8 2.0 constant_dynamic-slice_fusion.2
  252.0 12.5 %fusion.73 = (f32[4,16,128]{2,1,0:T(8,128)S(1)}, f32[4,16,128,640]{2,3,1,0:T(8,128)}) fusion(pred[128,640]{0,1:T(8,128)(4,1)S(1)} %fusion.72, bf16[1,128,4,16,128]{4,3,2,1,0:T(8,128)(2,1)S(1)} %constant_dynamic-slice_fusion.2, bf16[2,640,4,128]{1,3,2,0:T(8,128)(2,1)} %get-tuple-element.170, s32[]{:T(128)} %get-tuple-element.159), kind=kOutput, calls=%fused_computation.92.clone.1 | convolution fusion | flops 1363149440 | bytes 23839232 | tf_op jit(solution)/shard_map/while/body/eval_jaxpr/sub | solution.py:88
  264.5 10.4 %fusion.74 = bf16[4,128,16,128]{3,1,2,0:T(8,128)(2,1)} fusion(f32[4,16,128,640]{2,3,1,0:T(8,128)} %get-tuple-element.149, f32[4,16,128]{2,1,0:T(8,128)S(1)} %get-tuple-element.150, bf16[2,640,4,128]{1,3,2,0:T(8,128)(2,1)} %get-tuple-element.169, s32[]{:T(128)} %get-tuple-element.159), kind=kOutput, calls=%fused_computation.14.clone.1 | convolution fusion | flops 1353711616 | bytes 23757312 | tf_op jit(solution)/shard_map/while/body/eval_jaxpr/kgts,skd->tkgd/dot_general | solution.py:90
  275.0 2.9 %copy.61 = bf16[1,128,8192]{2,1,0:T(8,128)(2,1)S(1)} copy(bf16[1,128,8192]{1,2,0:T(8,128)(2,1)} %bitcast.131) | data formatting | bytes 4194304 | tf_op jit(solution)/shard_map/while/body/jit(dynamic_update_index_in_dim)/dynamic_update_slice | solution.py:95
  277.9 1.5 constant_dynamic-update-slice_fusion.2
  (37 shorter events, 4.0 us)
Async XLA Ops:
  6.5 55.0 %copy-start = (bf16[4,64,1024]{2,1,0:T(8,128)(2,1)S(1)}, bf16[4,64,1024]{2,1,0:T(8,128)(2,1)}, u32[]{:S(2)}) copy-start(bf16[4,64,1024]{2,1,0:T(8,128)(2,1)} %param.11) | copy-start | bytes 1572868
  6.5 200.1 %all-gather.3.cloned.1.call-start = ((), (), s32[]{:S(2)}) async-start(), calls=%async_computation.1 | async-start | bytes 8650752 | tf_op jit(solution)/shard_map/all_gather | solution.py:32
  68.9 8.1 %copy-start.5 = (s32[2,8]{1,0:T(2,128)S(1)}, s32[2,8]{1,0:T(2,128)}, u32[]{:S(2)}) copy-start(s32[2,8]{1,0:T(2,128)} %param.14) | copy-start | bytes 196
  68.9 8.3 %copy-start.2 = (bf16[2,8,16,4096]{3,2,1,0:T(8,128)(2,1)S(1)}, bf16[2,8,16,4096]{3,2,1,0:T(8,128)(2,1)}, u32[]{:S(2)}) copy-start(bf16[2,8,16,4096]{3,2,1,0:T(8,128)(2,1)} %param.12) | copy-start | bytes 6291460
  68.9 8.9 %copy-start.3 = (bf16[256,1024]{1,0:T(8,128)(2,1)S(1)}, bf16[256,1024]{1,0:T(8,128)(2,1)}, u32[]{:S(2)}) copy-start(bf16[256,1024]{1,0:T(8,128)(2,1)} %param.10) | copy-start | bytes 1572868
  68.9 134.8 %all-to-all-start = ((bf16[32,1,64,1024]{3,2,1,0:T(8,128)(2,1)}), bf16[32,1,64,1024]{3,2,1,0:T(8,128)(2,1)}, u32[]{:S(2)}, u32[]{:S(2)}) async-start(bf16[32,1,64,1024]{3,2,1,0:T(8,128)(2,1)} %bitcast_select_fusion.4), calls=%async_computation | async-start | bytes 8388608 | tf_op jit(solution)/shard_map/all_to_all | solution.py:55
  78.0 5.6 %copy-start.4 = (s32[2,8,16]{2,1,0:T(8,128)S(1)}, s32[2,8,16]{2,1,0:T(8,128)}, u32[]{:S(2)}) copy-start(s32[2,8,16]{2,1,0:T(8,128)} %param.15) | copy-start | bytes 3076
  279.4 1.0 copy-start.1
Sparse Core Ops, SparseCore 0:
  20.3 181.5 all-gather.2
where the time goes:
time: 288 us; the launch traced here: 287 us
  waiting for transfers between devices  118 us (41%)
  matrix products  55.1 us (19%)
  blocking collectives  53.9 us (19%)
  local copies, waits for them, and re-layouts  29.1 us (10%)
  between operations  13.5 us (5%)
  other arithmetic  9.49 us (3%)
  starting transfers between devices  8.12 us (3%)
    all_to_all x1, waiting for transfers between devices, local(): lax.all_to_all(outgoing, 'member', split_axis=0, concat_axis=0, tiled=True)  118 us
    all_gather x1, blocking collectives, local(): lax.all_gather(wanted.reshape(1, requests), 'member', axis=0, tiled=True)  40.2 us
    sub x2, matrix products, attend(): expd = jnp.exp(scores - peak)  25.1 us
    dot_general x2, matrix products, attend(): jnp.einsum('kgts,skd->tkgd', probs, value_block, preferred_element_type=j...  20.9 us
    all_gather x1, blocking collectives, local(): head_columns = lax.all_gather(w_kv, 'group', axis=1, tiled=True)  13.6 us
    dynamic_update_slice x4, local copies, waits for them, and re-layouts, local(): results = lax.map(attend, (queries, keys, values))  8.71 us
    all_to_all x1, starting transfers between devices, local(): lax.all_to_all(outgoing, 'member', split_axis=0, concat_axis=0, tiled=True)  8.12 us
    unnamed x14, local copies, waits for them, and re-layouts  7.19 us
  transfers between devices with their start and end apart: 2, of which 1 were waited for; matrix products, arithmetic and copies ran while one was open for 7% of the time, Pallas kernels for 0%

commit v1 on v0

--- a/solution.py
+++ b/solution.py
@@ -12,6 +12,12 @@
 PLEN = 64
 RECOMP = 16
 EPSILON = 1e-06
+
+
+def process_members_all_over_axis(xx, chip_axis, in_dim):
+    after = lax.axis_size(chip_axis)
+    k_now = jnp.concatenate([xx] * after, in_dim)
+    return lax.all_to_all(k_now, chip_axis, in_dim, in_dim, tiled=True)
 
 
 def local(q_rows, own_kv, cache, recomp_hidden, w_kv, retrieval, positions):
@@ -38,7 +44,7 @@
     holders_count = lax.axis_size("member")
     my_index = lax.axis_index("member")
     capacity = -(-requests // holders_count)
-    request_table = lax.all_gather(wanted.reshape(1, requests), "member", axis=0, tiled=True)
+    request_table = process_members_all_over_axis(wanted.reshape(1, requests), "member", 0)
     mine_mask = request_table // pass_local == my_index
     earlier_mask = (jnp.arange(requests)[:, None] < jnp.arange(requests)[None, :]).astype(jnp.int32)
     slot_rank = jnp.dot(mine_mask.astype(jnp.int32), earlier_mask)

time: 288 us -> 272 us (0.944)
  blocking collectives: 53.9 us -> 13.6 us
  waiting for transfers between devices: 118 us -> 131 us
  starting transfers between devices: 8.12 us -> 17.5 us
    all_gather x1 -> x0, blocking collectives: 40.2 us -> none  [local(): lax.all_gather(wanted.reshape(1, requests), 'member', axis=0, tiled=True)]
    all_to_all x0 -> x1, starting transfers between devices: none -> 11.4 us  [process_members_all_over_axis(): return lax.all_to_all(k_now, chip_axis, in_dim, in_dim, tiled=True)]
    all_to_all x0 -> x1, waiting for transfers between devices: none -> 8.6 us  [process_members_all_over_axis(): return lax.all_to_all(k_now, chip_axis, in_dim, in_dim, tiled=True)]
    all_to_all x1, waiting for transfers between devices: 118 us -> 123 us  [local(): lax.all_to_all(outgoing, 'member', split_axis=0, concat_axis=0, tiled=True)]
    unnamed x14 -> x13, local copies, waits for them, and re-layouts: 7.19 us -> 6.43 us
  transfers between devices with their start and end apart: 2 -> 3, of which waited for: 1 -> 2; matrix products, arithmetic and copies ran while one was open for 7% -> 8% of each run, Pallas kernels for 0% -> 0%
where the time goes in v1:
time: 272 us; the launch traced here: 270 us
  waiting for transfers between devices  131 us (48%)
  matrix products  55.1 us (20%)
  local copies, waits for them, and re-layouts  29.6 us (11%)
  starting transfers between devices  17.5 us (6%)
  blocking collectives  13.6 us (5%)
  between operations  13.5 us (5%)
  other arithmetic  9.49 us (3%)
    all_to_all x1, waiting for transfers between devices, local(): lax.all_to_all(outgoing, 'member', split_axis=0, concat_axis=0, tiled=True)  123 us
    sub x2, matrix products, attend(): expd = jnp.exp(scores - peak)  25.1 us
    dot_general x2, matrix products, attend(): jnp.einsum('kgts,skd->tkgd', probs, value_block, preferred_element_type=j...  20.9 us
    all_gather x1, blocking collectives, local(): head_columns = lax.all_gather(w_kv, 'group', axis=1, tiled=True)  13.6 us
    all_to_all x1, starting transfers between devices, process_members_all_over_axis(): return lax.all_to_all(k_now, chip_axis, in_dim, in_dim, tiled=True)  11.4 us
    dynamic_update_slice x4, local copies, waits for them, and re-layouts, local(): results = lax.map(attend, (queries, keys, values))  8.71 us
    all_to_all x1, waiting for transfers between devices, process_members_all_over_axis(): return lax.all_to_all(k_now, chip_axis, in_dim, in_dim, tiled=True)  8.6 us
    unnamed x13, local copies, waits for them, and re-layouts  6.43 us
  transfers between devices with their start and end apart: 3, of which 2 were waited for; matrix products, arithmetic and copies ran while one was open for 8% of the time, Pallas kernels for 0%

profile of v1, /device:TPU:32, one launch (start us, length us, event | category | flops | bytes accessed | tf_op | source)
XLA Modules:
  0.0 270.3 jit_solution(10718499953830397325)
XLA Ops:
  6.5 13.6 %all_gather.6 = bf16[128,1024]{1,0:T(8,128)(2,1)} all-gather(bf16[128,128]{1,0:T(8,128)(2,1)} %param.13), channel_id=1, replica_groups=mesh['group'=8,'member'=32] {'group'}, dimensions={1}, use_global_device_ids=true | all-gather | bytes 294912 | tf_op jit(solution)/shard_map/all_gather | solution.py:35
  21.6 11.4 %all-to-all-start = ((s32[32,1,16]{2,1,0:T(1,128)}), s32[32,1,16]{2,1,0:T(1,128)S(1)}, u32[]{:S(2)}, u32[]{:S(2)}) async-start(s32[32,1,16]{2,1,0:T(1,128)} %concatenate.9), calls=%async_computation | async-start | bytes 32768 | tf_op jit(solution)/shard_map/all_to_all | solution.py:20
  33.0 8.6 %all-to-all-done = s32[32,1,16]{2,1,0:T(1,128)S(1)} async-done(((s32[32,1,16]{2,1,0:T(1,128)}), s32[32,1,16]{2,1,0:T(1,128)S(1)}, u32[]{:S(2)}, u32[]{:S(2)}) %all-to-all-start) | async-done | bytes 2080 | tf_op jit(solution)/shard_map/all_to_all | solution.py:20
  41.9 2.8 %gather_fusion = bf16[32,64,1024]{2,1,0:T(8,128)(2,1)} fusion(bf16[4,64,1024]{2,1,0:T(8,128)(2,1)S(1)} %copy-done, s32[1024]{0:T(1024)S(1)} %pad_clamp_fusion.1), kind=kCustom, calls=%fused_computation | custom fusion | bytes 8388736 | tf_op jit(solution)/shard_map/gather | solution.py:59
  44.7 4.5 %bitcast_select_fusion.4 = bf16[32,1,64,1024]{3,2,1,0:T(8,128)(2,1)} fusion(bf16[32,64,1024]{2,1,0:T(8,128)(2,1)} %gather_fusion, pred[32]{0:T(512)(128)(4,1)S(1)} %reduce_or.19), kind=kLoop, calls=%fused_computation.31 | loop fusion | flops 2097152 | bytes 8388640 | tf_op jit(solution)/shard_map/jit(_where)/select_n | solution.py:58
  49.2 6.1 %all-to-all-start.1 = ((bf16[32,1,64,1024]{3,2,1,0:T(8,128)(2,1)}), bf16[32,1,64,1024]{3,2,1,0:T(8,128)(2,1)}, u32[]{:S(2)}, u32[]{:S(2)}) async-start(bf16[32,1,64,1024]{3,2,1,0:T(8,128)(2,1)} %bitcast_select_fusion.4), calls=%async_computation.1 | async-start | bytes 8388608 | tf_op jit(solution)/shard_map/all_to_all | solution.py:61
  56.3 5.4 %copy.43 = bf16[32,8,64,128]{3,2,1,0:T(8,128)(2,1)} copy(bf16[32,8,64,128]{3,1,2,0:T(8,128)(2,1)} %bitcast.134) | data formatting | bytes 8388608
  62.0 1.9 fusion.30
  64.0 122.8 %all-to-all-done.1 = bf16[32,1,64,1024]{3,2,1,0:T(8,128)(2,1)} async-done(((bf16[32,1,64,1024]{3,2,1,0:T(8,128)(2,1)}), bf16[32,1,64,1024]{3,2,1,0:T(8,128)(2,1)}, u32[]{:S(2)}, u32[]{:S(2)}) %all-to-all-start.1) | async-done | bytes 4194336 | tf_op jit(solution)/shard_map/all_to_all | solution.py:61
  186.8 2.9 %gather_fusion.1 = bf16[16,64,1024]{2,1,0:T(8,128)(2,1)S(1)} fusion(bf16[32,64,1024]{2,1,0:T(8,128)(2,1)} %bitcast.7, s32[1024]{0:T(1024)S(1)} %pad_clamp_fusion), kind=kCustom, calls=%fused_computation.1 | custom fusion | bytes 4194368 | tf_op jit(solution)/shard_map/gather | solution.py:66
  189.7 6.3 %convolution_convert_fusion = bf16[256,1024]{1,0:T(8,128)(2,1)S(1)} fusion(bf16[256,4096]{1,0:T(8,128)(2,1)} %fusion.30, bf16[4096,1024]{1,0:T(8,128)(2,1)} %all-gather.2.cloned.1.call-done), kind=kOutput, calls=%fused_computation.40 | convolution fusion | flops 2147745792 | bytes 11010048 | tf_op jit(solution)/shard_map/dot_general | solution.py:36
  196.1 2.6 convert_select_fusion
  198.6 2.9 %copy.31 = bf16[2,512,1024]{1,2,0:T(8,128)(2,1)S(1)} copy(bf16[2,512,1024]{2,1,0:T(8,128)(2,1)} %bitcast.133) | data formatting | bytes 4194304 | tf_op jit(solution)/shard_map/reshape | solution.py:75
  201.5 1.7 pad_maximum_fusion
  203.2 59.2 %while.11 = (s32[]{:T(128)}, bf16[2,128,8192]{2,1,0:T(8,128)(2,1)}, bf16[2,640,4,128]{1,3,2,0:T(8,128)(2,1)}, bf16[2,640,4,128]{1,3,2,0:T(8,128)(2,1)}, bf16[2,1...) while((s32[]{:T(128)}, bf16[2,128,8192]{2,1,0:T(8,128)(2,1)}, ...), condition=%wide.region_8.9_spmd.clone, body=%wide.region_5.8_spmd.clone.sunk | while | flops 2717024768 | bytes 60265176 | solution.py:101
  203.2 2.0 constant_dynamic-slice_fusion.2
  205.5 12.5 %fusion.73 = (f32[4,16,128]{2,1,0:T(8,128)S(1)}, f32[4,16,128,640]{2,3,1,0:T(8,128)}) fusion(pred[128,640]{0,1:T(8,128)(4,1)S(1)} %fusion.72, bf16[1,128,4,16,128]{4,3,2,1,0:T(8,128)(2,1)S(1)} %constant_dynamic-slice_fusion.2, bf16[2,640,4,128]{1,3,2,0:T(8,128)(2,1)} %get-tuple-element.170, s32[]{:T(128)} %get-tuple-element.159), kind=kOutput, calls=%fused_computation.92.clone.1 | convolution fusion | flops 1363149440 | bytes 23839232 | tf_op jit(solution)/shard_map/while/body/eval_jaxpr/sub | solution.py:94
  218.0 10.4 %fusion.74 = bf16[4,128,16,128]{3,1,2,0:T(8,128)(2,1)} fusion(f32[4,16,128,640]{2,3,1,0:T(8,128)} %get-tuple-element.149, f32[4,16,128]{2,1,0:T(8,128)S(1)} %get-tuple-element.150, bf16[2,640,4,128]{1,3,2,0:T(8,128)(2,1)} %get-tuple-element.169, s32[]{:T(128)} %get-tuple-element.159), kind=kOutput, calls=%fused_computation.14.clone.1 | convolution fusion | flops 1353711616 | bytes 23757312 | tf_op jit(solution)/shard_map/while/body/eval_jaxpr/kgts,skd->tkgd/dot_general | solution.py:96
  228.5 2.9 %copy.58 = bf16[1,128,8192]{2,1,0:T(8,128)(2,1)S(1)} copy(bf16[1,128,8192]{1,2,0:T(8,128)(2,1)} %bitcast.131) | data formatting | bytes 4194304 | tf_op jit(solution)/shard_map/while/body/jit(dynamic_update_index_in_dim)/dynamic_update_slice | solution.py:101
  231.4 1.5 constant_dynamic-update-slice_fusion.2
  232.8 2.0 constant_dynamic-slice_fusion.2
  235.1 12.5 %fusion.73 = (f32[4,16,128]{2,1,0:T(8,128)S(1)}, f32[4,16,128,640]{2,3,1,0:T(8,128)}) fusion(pred[128,640]{0,1:T(8,128)(4,1)S(1)} %fusion.72, bf16[1,128,4,16,128]{4,3,2,1,0:T(8,128)(2,1)S(1)} %constant_dynamic-slice_fusion.2, bf16[2,640,4,128]{1,3,2,0:T(8,128)(2,1)} %get-tuple-element.170, s32[]{:T(128)} %get-tuple-element.159), kind=kOutput, calls=%fused_computation.92.clone.1 | convolution fusion | flops 1363149440 | bytes 23839232 | tf_op jit(solution)/shard_map/while/body/eval_jaxpr/sub | solution.py:94
  247.6 10.4 %fusion.74 = bf16[4,128,16,128]{3,1,2,0:T(8,128)(2,1)} fusion(f32[4,16,128,640]{2,3,1,0:T(8,128)} %get-tuple-element.149, f32[4,16,128]{2,1,0:T(8,128)S(1)} %get-tuple-element.150, bf16[2,640,4,128]{1,3,2,0:T(8,128)(2,1)} %get-tuple-element.169, s32[]{:T(128)} %get-tuple-element.159), kind=kOutput, calls=%fused_computation.14.clone.1 | convolution fusion | flops 1353711616 | bytes 23757312 | tf_op jit(solution)/shard_map/while/body/eval_jaxpr/kgts,skd->tkgd/dot_general | solution.py:96
  258.1 2.9 %copy.58 = bf16[1,128,8192]{2,1,0:T(8,128)(2,1)S(1)} copy(bf16[1,128,8192]{1,2,0:T(8,128)(2,1)} %bitcast.131) | data formatting | bytes 4194304 | tf_op jit(solution)/shard_map/while/body/jit(dynamic_update_index_in_dim)/dynamic_update_slice | solution.py:101
  (38 shorter events, 6.0 us)
Async XLA Ops:
  6.5 35.3 %copy-start = (bf16[4,64,1024]{2,1,0:T(8,128)(2,1)S(1)}, bf16[4,64,1024]{2,1,0:T(8,128)(2,1)}, u32[]{:S(2)}) copy-start(bf16[4,64,1024]{2,1,0:T(8,128)(2,1)} %param.11) | copy-start | bytes 1572868
  6.5 183.2 %all-gather.2.cloned.1.call-start = ((), (), s32[]{:S(2)}) async-start(), calls=%async_computation.2 | async-start | bytes 8650752 | tf_op jit(solution)/shard_map/all_gather | solution.py:38
  21.6 20.0 %all-to-all-start = ((s32[32,1,16]{2,1,0:T(1,128)}), s32[32,1,16]{2,1,0:T(1,128)S(1)}, u32[]{:S(2)}, u32[]{:S(2)}) async-start(s32[32,1,16]{2,1,0:T(1,128)} %concatenate.9), calls=%async_computation | async-start | bytes 32768 | tf_op jit(solution)/shard_map/all_to_all | solution.py:20
  49.2 6.1 %copy-start.5 = (s32[2,8]{1,0:T(2,128)S(1)}, s32[2,8]{1,0:T(2,128)}, u32[]{:S(2)}) copy-start(s32[2,8]{1,0:T(2,128)} %param.14) | copy-start | bytes 196
  49.2 6.2 %copy-start.2 = (bf16[2,8,16,4096]{3,2,1,0:T(8,128)(2,1)S(1)}, bf16[2,8,16,4096]{3,2,1,0:T(8,128)(2,1)}, u32[]{:S(2)}) copy-start(bf16[2,8,16,4096]{3,2,1,0:T(8,128)(2,1)} %param.12) | copy-start | bytes 6291460
  49.2 6.8 %copy-start.3 = (bf16[256,1024]{1,0:T(8,128)(2,1)S(1)}, bf16[256,1024]{1,0:T(8,128)(2,1)}, u32[]{:S(2)}) copy-start(bf16[256,1024]{1,0:T(8,128)(2,1)} %param.10) | copy-start | bytes 1572868
  49.2 137.6 %all-to-all-start.1 = ((bf16[32,1,64,1024]{3,2,1,0:T(8,128)(2,1)}), bf16[32,1,64,1024]{3,2,1,0:T(8,128)(2,1)}, u32[]{:S(2)}, u32[]{:S(2)}) async-start(bf16[32,1,64,1024]{3,2,1,0:T(8,128)(2,1)} %bitcast_select_fusion.4), calls=%async_computation.1 | async-start | bytes 8388608 | tf_op jit(solution)/shard_map/all_to_all | solution.py:61
  56.3 5.6 %copy-start.4 = (s32[2,8,16]{2,1,0:T(8,128)S(1)}, s32[2,8,16]{2,1,0:T(8,128)}, u32[]{:S(2)}) copy-start(s32[2,8,16]{2,1,0:T(8,128)} %param.15) | copy-start | bytes 3076
  262.4 1.0 copy-start.1
Sparse Core Ops, SparseCore 0:
  20.3 167.9 all-gather.1
